TPU v7x, 128 devices: a whole 4x4x4 slice. The times are simulated.
128 devices in a mesh: gx: 16 (over y, x), gy: 8 (over z, core).
Axes of the slice: x: 4, y: 4, z: 4, core: 2. Of those that a mesh axis runs over, the one named last changes fastest.
Arguments:
- prior_member_matrix: float32 [8, 256, 256, 128], P(None, 'gx', 'gy'), may hold values from -6 to 6
- east_speed: float32 [4, 256, 256], P(None, 'gx', 'gy'), may hold values from -0.3 to 0.3
- north_speed: float32 [4, 256, 256], P(None, 'gx', 'gy'), may hold values from -0.3 to 0.3
- diffusion: float32 [4, 256, 256], P(None, 'gx', 'gy'), may hold values from 0.1 to 0.22
- obs_column: int32 [1024, 2], replicated, may hold values from 0 to 255, as said below
- obs_comp: int32 [1024], replicated, may hold values from 0 to 7
- observation_reach: int32 [1024], replicated, may hold values from 0 to 3
- obs_owner: int32 [1024], replicated, may hold values from 0 to 15, as said below
- obs_order: int32 [1024], replicated, may hold values from 0 to 1023, each once
- obs_value: float32 [16, 8, 32], P('gx', 'gy'), may hold values from -6 to 6
- obs_error: float32 [16, 8, 32], P('gx', 'gy'), may hold values from 0.3 to 3
Outputs:
- analysis: float32 [8, 256, 256, 128], P(None, 'gx', 'gy')
Inputs may be any that keep to these rules, and one draw needn't show every extreme that they name: `obs_column`: tile t = (8 tx + ty) holds observations 8 t to 8 (t + 1) - 1; each entry is a (longitude, latitude) column inside that tile. `obs_owner`: the owner lies in the observation's latitude tile; one tile's observations reach one owner at most 2 times, and exactly 2 times for some owner of every tile.
All inputs are finite; a program needn't handle non-finite values.
Results may differ from a plain program's by a relative error of at most 0.0001.
Values sent between devices are 32-bit elements; how exact they have to be, the bound alone decides.
No kernel may reach another device: no remote copies, remote signals or barrier semaphores. Data moves between devices by JAX's collectives and lax.ppermute only.
A program may use at most 64 MiB of HBM per device.

v0:
```python
import jax
import jax.numpy as jnp
from jax import lax
from jax.sharding import PartitionSpec as P

FSTEPS = 2
PANEL = 256
PRECISE = lax.Precision.HIGHEST


def with_halo(cells, sides, width, closed):
    for axis, dim in sides:
        count = lax.axis_size(axis)
        ends = count if closed else count - 1
        head = lax.slice_in_dim(cells, 0, width, axis=dim)
        tail = lax.slice_in_dim(cells, cells.shape[dim] - width, cells.shape[dim], axis=dim)
        cells = jnp.concatenate(
            [
                lax.ppermute(tail, axis, [(i, (i + 1) % count) for i in range(ends)]),
                cells,
                lax.ppermute(head, axis, [((i + 1) % count, i) for i in range(ends)]),
            ],
            axis=dim,
        )
    return cells


def slot_rank(tile_x, tile_y, owner, tiles_x, tiles_y):
    total_obs = owner.shape[0]
    keyed = (tile_x * tiles_y + tile_y) * tiles_x + owner
    sort_order = jnp.argsort(keyed, stable=True)
    sorted_keys = keyed[sort_order]
    places = jnp.arange(total_obs, dtype=jnp.int32)
    segment_beginning = jnp.concatenate(
        [jnp.ones((1,), dtype=bool), sorted_keys[1:] != sorted_keys[:-1]]
    )
    starts = lax.cummax(jnp.where(segment_beginning, places, 0), axis=0)
    ranked = places - starts
    inverse_order = jnp.argsort(sort_order)
    return ranked[inverse_order]


def horizontal(first_x, first_y, second_x, second_y, span_x, span_y, total_x):
    wrapped = (first_x - second_x) % total_x
    dist_x = jnp.minimum(wrapped, total_x - wrapped).astype(jnp.float32)
    dist_y = (first_y - second_y).astype(jnp.float32)
    radius_sq = (dist_x / span_x) ** 2 + (dist_y / span_y) ** 2
    return jnp.maximum(0.0, 1.0 - radius_sq) ** 2


def vertical(first_level, second_level, reach):
    level_gap = jnp.abs(first_level - second_level).astype(jnp.float32)
    return jnp.maximum(0.0, 1.0 - level_gap / (reach.astype(jnp.float32) + 1.0))


def panel_terms(priors, values, errors):
    members = priors.shape[1]
    centre = jnp.mean(priors, axis=1)
    spread = priors - centre[:, None]
    variance = jnp.sum(spread * spread, axis=1) / (members - 1)
    inverse = 1.0 / (variance + errors)
    damping = 1.0 / (1.0 + jnp.sqrt(errors * inverse))
    return (spread, (values - centre) * inverse, damping * inverse)


def regress(row_block, weight, spread, mean_gain, shrink):
    members = row_block.shape[1]
    centre = jnp.mean(row_block, axis=1, keepdims=True)
    anomaly = row_block - centre
    covariance = jnp.dot(
        anomaly, spread.T, precision=PRECISE, preferred_element_type=jnp.float32
    ) / (members - 1)
    weighted = weight * covariance
    centre = centre + jnp.dot(
        weighted, mean_gain[:, None], precision=PRECISE, preferred_element_type=jnp.float32
    )
    anomaly = anomaly - jnp.dot(
        weighted * shrink[None, :], spread, precision=PRECISE, preferred_element_type=jnp.float32
    )
    return centre + anomaly


def shards(
    prior_member_matrix,
    east_speed,
    north_speed,
    diffusion,
    obs_column,
    obs_comp,
    observation_reach,
    obs_owner,
    obs_order,
    obs_value,
    obs_error,
):
    comps, zonal_extent, width_y, members = prior_member_matrix.shape
    per_level = comps // east_speed.shape[0]
    tiles_x = lax.axis_size("gx")
    tiles_y = lax.axis_size("gy")
    here_x = lax.axis_index("gx")
    here_y = lax.axis_index("gy")
    east_vel = jnp.repeat(east_speed, per_level, axis=0)[..., None]
    north_vel = jnp.repeat(north_speed, per_level, axis=0)[..., None]
    diff_coef = jnp.repeat(diffusion, per_level, axis=0)[..., None]
    model_mesh_values = prior_member_matrix
    for substep in range(FSTEPS):
        rim_wide = with_halo(model_mesh_values, (("gx", 1),), 1, True)
        rim_tall = with_halo(model_mesh_values, (("gy", 2),), 1, False)
        east_side = rim_wide[:, 2:]
        west_side = rim_wide[:, :-2]
        north_side = rim_tall[:, :, 2:]
        south_side = rim_tall[:, :, :-2]
        spread_term = diff_coef * (
            east_side + west_side + north_side + south_side - 4.0 * model_mesh_values
        )
        carry_term = 0.5 * (
            east_vel * (east_side - west_side) + north_vel * (north_side - south_side)
        )
        model_mesh_values = model_mesh_values + spread_term - carry_term
    row_state = model_mesh_values.reshape(comps * zonal_extent * width_y, members)
    obs_total = obs_comp.shape[0]
    slot_count = obs_value.shape[2]
    capacity = slot_count // tiles_x
    panel_count = obs_total // PANEL
    col_x = obs_column[:, 0]
    col_y = obs_column[:, 1]
    tile_x = col_x // zonal_extent
    tile_y = col_y // width_y
    ranked_slot = slot_rank(tile_x, tile_y, obs_owner, tiles_x, tiles_y)
    obs_level = obs_comp // per_level
    in_tile = (tile_x == here_x) & (tile_y == here_y)
    held_here = (obs_owner == here_x) & (tile_y == here_y)
    own_place = tile_x * capacity + ranked_slot
    element = (
        (obs_comp * zonal_extent + col_x - tile_x * zonal_extent) * width_y
        + col_y
        - tile_y * width_y
    )
    total_x = zonal_extent * tiles_x
    grid_x = jnp.repeat(here_x * zonal_extent + jnp.arange(zonal_extent, dtype=jnp.int32), width_y)
    grid_y = jnp.tile(here_y * width_y + jnp.arange(width_y, dtype=jnp.int32), zonal_extent)
    comp_level = jnp.arange(comps, dtype=jnp.int32) // per_level
    local_vals = obs_value.reshape(slot_count)
    local_errs = obs_error.reshape(slot_count)

    def state_weight(panel_index_list):
        flat_weight = horizontal(
            grid_x[:, None],
            grid_y[:, None],
            col_x[panel_index_list][None, :],
            col_y[panel_index_list][None, :],
            3.0 * zonal_extent,
            3.0 * width_y,
            total_x,
        )
        level_weight = vertical(
            comp_level[:, None],
            obs_level[panel_index_list][None, :],
            observation_reach[panel_index_list][None, :],
        )
        return (level_weight[:, None, :] * flat_weight[None, :, :]).reshape(
            -1, panel_index_list.shape[0]
        )

    slot_ids = jnp.arange(slot_count, dtype=jnp.int32)
    measurement_labels = jnp.arange(obs_total, dtype=jnp.int32)
    send_place = obs_owner * capacity + ranked_slot
    send_match = in_tile[None, :] & (send_place[None, :] == slot_ids[:, None])
    filled = jnp.any(send_match, axis=1)
    source_elem = jnp.sum(jnp.where(send_match, element[None, :], 0), axis=1)
    outgoing = jnp.where(filled[:, None], row_state[source_elem], 0.0).reshape(
        tiles_x, capacity, members
    )
    arrived = lax.all_to_all(outgoing, "gx", split_axis=0, concat_axis=0, tiled=True).reshape(
        slot_count, members
    )
    hold_match = held_here[None, :] & (own_place[None, :] == slot_ids[:, None])
    held_obs = jnp.sum(jnp.where(hold_match, measurement_labels[None, :], 0), axis=1)
    slot_east_coord = col_x[held_obs]
    slot_y = col_y[held_obs]
    slot_level = obs_level[held_obs]
    all_vals, all_errs = (
        lax.all_gather(local_vals, ("gx", "gy"), axis=0, tiled=True),
        lax.all_gather(local_errs, ("gx", "gy"), axis=0, tiled=True),
    )
    global_place = (obs_owner * tiles_y + tile_y) * slot_count + own_place
    obs_vals = all_vals[global_place]
    obs_errs = all_errs[global_place]

    def one_panel(panel_num, carried):
        row_state, owner_rows = carried
        panel_index_list = lax.dynamic_slice_in_dim(obs_order, panel_num * PANEL, PANEL)
        every_slot = lax.all_gather(owner_rows, ("gx", "gy"), axis=0, tiled=True)
        priors = every_slot[global_place[panel_index_list]]
        spread, mean_gain, shrink = panel_terms(
            priors, obs_vals[panel_index_list], obs_errs[panel_index_list]
        )
        owner_weight = horizontal(
            slot_east_coord[:, None],
            slot_y[:, None],
            col_x[panel_index_list][None, :],
            col_y[panel_index_list][None, :],
            3.0 * zonal_extent,
            3.0 * width_y,
            total_x,
        )
        owner_weight = owner_weight * vertical(
            slot_level[:, None],
            obs_level[panel_index_list][None, :],
            observation_reach[panel_index_list][None, :],
        )
        new_state = regress(row_state, state_weight(panel_index_list), spread, mean_gain, shrink)
        new_owner = regress(owner_rows, owner_weight, spread, mean_gain, shrink)
        return (new_state, new_owner)

    row_state, owner_rows = lax.fori_loop(0, panel_count, one_panel, (row_state, arrived))
    return row_state.reshape(comps, zonal_extent, width_y, members)


def solution(mesh):
    return jax.shard_map(
        shards,
        mesh=mesh,
        in_specs=(
            P(None, "gx", "gy", None),
            P(None, "gx", "gy"),
            P(None, "gx", "gy"),
            P(None, "gx", "gy"),
            P(),
            P(),
            P(),
            P(),
            P(),
            P("gx", "gy", None),
            P("gx", "gy", None),
        ),
        out_specs=P(None, "gx", "gy", None),
        check_vma=False,
    )
```

profile of v0, /device:TPU:1, one launch (start us, length us, event | category | flops | bytes accessed | tf_op | source)
XLA Modules:
  0.0 494.7 jit_solution(18060016406997314425)
XLA Ops:
  7.8 3.3 collective-permute-start.2
  11.2 3.5 collective-permute-start.3
  17.0 3.8 collective-permute-start
  23.0 4.4 sort.34
  27.4 4.5 gather_fusion.8
  32.0 4.4 sort.35
  37.0 4.5 gather_fusion.9
  43.7 64.4 %all-reduce.2 = (f32[4096]{0:T(1024)S(1)}, f32[4096]{0:T(1024)S(1)}) all-reduce(f32[4096]{0:T(1024)S(1)} %bitcast_dynamic-update-slice_fusion.1, f32[4096]{0:T(1024)S(1)} %bitcast_dynamic-update-slice_fusion), channel_id=2, replica_groups=mesh['gx'=16,'gy'=8] {'gx','gy'}, use_global_device_ids=true, to_apply=%add | all-reduce | flops 8192 | bytes 65536 | tf_op jit(solution)/shard_map/all_gather | solution.py:183
  108.0 6.1 %gather_fusion.12 = f32[1024]{0:T(1024)S(1)} fusion(f32[4096]{0:T(1024)S(1)} %get-tuple-element.561, s32[1024]{0:T(1024)S(1)} %get-tuple-element.564), kind=kCustom, calls=%fused_computation.12 | custom fusion | bytes 12288 | tf_op jit(solution)/shard_map/gather | solution.py:188
  114.2 6.2 %gather_fusion.11 = f32[1024]{0:T(1024)S(1)} fusion(f32[4096]{0:T(1024)S(1)} %get-tuple-element.560, s32[1024]{0:T(1024)S(1)} %get-tuple-element.564), kind=kCustom, calls=%fused_computation.11 | custom fusion | bytes 12288 | tf_op jit(solution)/shard_map/gather | solution.py:187
  121.3 2.2 multiply_subtract_fusion.1
  123.9 4.5 collective-permute-start.4
  128.5 3.1 collective-permute-start.6
  131.6 2.5 collective-permute-start.7
  135.4 2.1 multiply_subtract_fusion
  138.8 3.5 all-to-all-start
  142.9 5.8 %all-to-all-done = f32[16,2,128]{2,1,0:T(2,128)S(1)} async-done(((f32[16,2,128]{2,1,0:T(2,128)}), f32[16,2,128]{2,1,0:T(2,128)S(1)}, u32[]{:S(2)}, u32[]{:S(2)}) %all-to-all-start) | async-done | bytes 16416 | tf_op jit(solution)/shard_map/all_to_all | solution.py:174
  148.7 338.1 %while.18 = (s32[]{:T(128)}, f32[4096,128]{1,0:T(8,128)S(1)}, f32[32,128]{1,0:T(8,128)S(1)}, s32[1024]{0:T(1024)}, s32[1024]{0:T(1024)S(1)}, /*index=5*/s32[1024...) while((s32[]{:T(128)}, f32[4096,128]{1,0:T(8,128)S(1)}, ...), condition=%wide.region_12.13_spmd.clone, body=%wide.region_7.12_spmd.clone.sunk | while | flops 3269761536 | bytes 36260832 | solution.py:216
  152.4 1.4 gather_fusion.3
  153.8 1.4 gather_fusion.2
  155.2 1.4 gather_fusion.7
  156.5 1.4 gather_fusion.6
  157.9 1.4 gather_fusion.4
  159.3 1.4 gather_fusion
  161.5 2.3 broadcast_multiply_fusion.9
  163.8 54.0 %all-gather.4.cloned.1.call-done = f32[4096,128]{1,0:T(8,128)} async-done(((f32[32,128]{1,0:T(8,128)}), f32[4096,128]{1,0:T(8,128)}) %all-gather.4.cloned.1.call-update) | async-done | bytes 2097168 | tf_op jit(solution)/shard_map/while/body/eval_jaxpr/all_gather | solution.py:193
  217.8 2.3 gather_fusion.1
  220.9 5.6 %fusion.99 = f32[4096,256]{1,0:T(8,128)S(1)} fusion(f32[4096,256]{1,0:T(8,128)} %bitcast.72, f32[4096,128]{1,0:T(8,128)S(1)} %get-tuple-element.720, f32[4096]{0:T(1024)S(1)} %broadcast_multiply_fusion.10, f32[256,128]{1,0:T(8,128)S(1)} %gather_fusion.1, f32[256]{0:T(256)S(1)} %broadcast_multiply_fusion.8), kind=kOutput, calls=%fused_computation.20.clone.1 | convolution fusion | flops 1613266944 | bytes 10634240 | tf_op jit(solution)/shard_map/while/body/eval_jaxpr/dot_general | solution.py:70
  226.5 3.6 fusion.100
  230.4 4.6 fusion.102
  238.8 1.4 gather_fusion.3
  240.2 1.4 gather_fusion.2
  241.6 1.4 gather_fusion.7
  242.9 1.4 gather_fusion.6
  244.3 1.4 gather_fusion.4
  245.7 1.4 gather_fusion
  248.0 2.3 broadcast_multiply_fusion.9
  250.3 51.6 %all-gather.4.cloned.1.call-done = f32[4096,128]{1,0:T(8,128)} async-done(((f32[32,128]{1,0:T(8,128)}), f32[4096,128]{1,0:T(8,128)}) %all-gather.4.cloned.1.call-update) | async-done | bytes 2097168 | tf_op jit(solution)/shard_map/while/body/eval_jaxpr/all_gather | solution.py:193
  301.9 2.3 gather_fusion.1
  305.0 5.6 %fusion.99 = f32[4096,256]{1,0:T(8,128)S(1)} fusion(f32[4096,256]{1,0:T(8,128)} %bitcast.72, f32[4096,128]{1,0:T(8,128)S(1)} %get-tuple-element.720, f32[4096]{0:T(1024)S(1)} %broadcast_multiply_fusion.10, f32[256,128]{1,0:T(8,128)S(1)} %gather_fusion.1, f32[256]{0:T(256)S(1)} %broadcast_multiply_fusion.8), kind=kOutput, calls=%fused_computation.20.clone.1 | convolution fusion | flops 1613266944 | bytes 10634240 | tf_op jit(solution)/shard_map/while/body/eval_jaxpr/dot_general | solution.py:70
  310.5 3.6 fusion.100
  314.5 4.6 fusion.102
  322.8 1.4 gather_fusion.3
  324.2 1.4 gather_fusion.2
  325.6 1.4 gather_fusion.7
  327.0 1.4 gather_fusion.6
  328.3 1.4 gather_fusion.4
  329.7 1.4 gather_fusion
  332.0 2.3 broadcast_multiply_fusion.9
  334.3 51.6 %all-gather.4.cloned.1.call-done = f32[4096,128]{1,0:T(8,128)} async-done(((f32[32,128]{1,0:T(8,128)}), f32[4096,128]{1,0:T(8,128)}) %all-gather.4.cloned.1.call-update) | async-done | bytes 2097168 | tf_op jit(solution)/shard_map/while/body/eval_jaxpr/all_gather | solution.py:193
  385.9 2.3 gather_fusion.1
  389.0 5.6 %fusion.99 = f32[4096,256]{1,0:T(8,128)S(1)} fusion(f32[4096,256]{1,0:T(8,128)} %bitcast.72, f32[4096,128]{1,0:T(8,128)S(1)} %get-tuple-element.720, f32[4096]{0:T(1024)S(1)} %broadcast_multiply_fusion.10, f32[256,128]{1,0:T(8,128)S(1)} %gather_fusion.1, f32[256]{0:T(256)S(1)} %broadcast_multiply_fusion.8), kind=kOutput, calls=%fused_computation.20.clone.1 | convolution fusion | flops 1613266944 | bytes 10634240 | tf_op jit(solution)/shard_map/while/body/eval_jaxpr/dot_general | solution.py:70
  394.6 3.6 fusion.100
  398.5 4.6 fusion.102
  406.8 1.4 gather_fusion.3
  408.1 1.4 gather_fusion.2
  409.5 1.4 gather_fusion.7
  410.9 1.4 gather_fusion.6
  415.9 2.3 broadcast_multiply_fusion.9
  418.2 51.4 %all-gather.4.cloned.1.call-done = f32[4096,128]{1,0:T(8,128)} async-done(((f32[32,128]{1,0:T(8,128)}), f32[4096,128]{1,0:T(8,128)}) %all-gather.4.cloned.1.call-update) | async-done | bytes 2097168 | tf_op jit(solution)/shard_map/while/body/eval_jaxpr/all_gather | solution.py:193
  469.6 2.3 gather_fusion.1
  472.7 5.6 %fusion.99 = f32[4096,256]{1,0:T(8,128)S(1)} fusion(f32[4096,256]{1,0:T(8,128)} %bitcast.72, f32[4096,128]{1,0:T(8,128)S(1)} %get-tuple-element.720, f32[4096]{0:T(1024)S(1)} %broadcast_multiply_fusion.10, f32[256,128]{1,0:T(8,128)S(1)} %gather_fusion.1, f32[256]{0:T(256)S(1)} %broadcast_multiply_fusion.8), kind=kOutput, calls=%fused_computation.20.clone.1 | convolution fusion | flops 1613266944 | bytes 10634240 | tf_op jit(solution)/shard_map/while/body/eval_jaxpr/dot_general | solution.py:70
  478.3 3.6 fusion.100
  482.2 4.6 fusion.102
  (194 shorter events, 39.4 us)
Async XLA Ops:
  7.8 113.3 %collective-permute-start.2 = (f32[8,16,1,128]{3,2,1,0:T(1,128)S(1)}, f32[8,16,1,128]{3,2,1,0:T(1,128)S(1)}, u32[]{:S(2)}, u32[]{:S(2)}) collective-permute-start(f32[8,16,1,128]{3,2,1,0:T(1,128)S(1)} %get-tuple-element.577), channel_id=1, source_target_pairs={{1,0},{2,1},{3,2},{4,3},{5,4},{6,5},{7,6},{9,8},{10,9},{11,10},{12... | collective-permute-start | bytes 196616 | tf_op jit(solution)/shard_map/ppermute | solution.py:21
  11.2 110.0 %collective-permute-start.3 = (f32[8,16,1,128]{3,2,1,0:T(1,128)S(1)}, f32[8,16,1,128]{3,2,1,0:T(1,128)S(1)}, u32[]{:S(2)}, u32[]{:S(2)}) collective-permute-start(f32[8,16,1,128]{3,2,1,0:T(1,128)S(1)} %get-tuple-element.578), channel_id=1, source_target_pairs={{0,1},{1,2},{2,3},{3,4},{4,5},{5,6},{6,7},{8,9},{9,10},{10,11},{11... | collective-permute-start | bytes 196616 | tf_op jit(solution)/shard_map/ppermute | solution.py:19
  15.7 105.5 %collective-permute-start.1 = (f32[8,1,32,128]{3,2,1,0:T(8,128)S(1)}, f32[8,1,32,128]{3,2,1,0:T(8,128)S(1)}, u32[]{:S(2)}, u32[]{:S(2)}) collective-permute-start(f32[8,1,32,128]{3,2,1,0:T(8,128)S(1)} %get-tuple-element.575), channel_id=1, source_target_pairs={{0,8},{8,16},{16,24},{24,32},{32,40},{40,48},{48,56},{56,64},{64,7... | collective-permute-start | bytes 393224 | tf_op jit(solution)/shard_map/ppermute | solution.py:19
  17.0 104.2 %collective-permute-start = (f32[8,1,32,128]{3,2,1,0:T(8,128)S(1)}, f32[8,1,32,128]{3,2,1,0:T(8,128)S(1)}, u32[]{:S(2)}, u32[]{:S(2)}) collective-permute-start(f32[8,1,32,128]{3,2,1,0:T(8,128)S(1)} %get-tuple-element.576), channel_id=1, source_target_pairs={{8,0},{16,8},{24,16},{32,24},{40,32},{48,40},{56,48},{64,56},{72,6... | collective-permute-start | bytes 393224 | tf_op jit(solution)/shard_map/ppermute | solution.py:21
  37.0 4.6 copy-start.5
  37.0 4.6 copy-start.9
  37.0 5.0 %copy-start.10 = (f32[1,1,32]{2,1,0:T(1,128)S(1)}, f32[1,1,32]{2,1,0:T(1,128)}, u32[]{:S(2)}) copy-start(f32[1,1,32]{2,1,0:T(1,128)} %param.22) | copy-start | bytes 388
  37.0 5.2 %copy-start.11 = (f32[1,1,32]{2,1,0:T(1,128)S(1)}, f32[1,1,32]{2,1,0:T(1,128)}, u32[]{:S(2)}) copy-start(f32[1,1,32]{2,1,0:T(1,128)} %param.23) | copy-start | bytes 388
  114.2 7.0 %copy-start.6 = (f32[4,16,32]{2,1,0:T(8,128)S(1)}, f32[4,16,32]{2,1,0:T(8,128)}, u32[]{:S(2)}) copy-start(f32[4,16,32]{2,1,0:T(8,128)} %param.14) | copy-start | bytes 24580
  114.2 7.0 %copy-start.7 = (f32[4,16,32]{2,1,0:T(8,128)S(1)}, f32[4,16,32]{2,1,0:T(8,128)}, u32[]{:S(2)}) copy-start(f32[4,16,32]{2,1,0:T(8,128)} %param.15) | copy-start | bytes 24580
  114.2 7.1 %copy-start.8 = (f32[4,16,32]{2,1,0:T(8,128)S(1)}, f32[4,16,32]{2,1,0:T(8,128)}, u32[]{:S(2)}) copy-start(f32[4,16,32]{2,1,0:T(8,128)} %param.16) | copy-start | bytes 24580
  114.2 7.1 %copy-start.4 = (f32[8,16,32,128]{3,2,1,0:T(8,128)S(1)}, f32[8,16,32,128]{3,2,1,0:T(8,128)}, u32[]{:S(2)}) copy-start(f32[8,16,32,128]{3,2,1,0:T(8,128)} %param.13) | copy-start | bytes 6291460
  123.6 11.8 %collective-permute-start.5 = (f32[8,1,32,128]{3,2,1,0:T(8,128)S(1)}, f32[8,1,32,128]{3,2,1,0:T(8,128)S(1)}, u32[]{:S(2)}, u32[]{:S(2)}) collective-permute-start(f32[8,1,32,128]{3,2,1,0:T(8,128)S(1)} %get-tuple-element.571), channel_id=1, source_target_pairs={{0,8},{8,16},{16,24},{24,32},{32,40},{40,48},{48,56},{56,64},{64,7... | collective-permute-start | bytes 393224 | tf_op jit(solution)/shard_map/ppermute | solution.py:19
  123.9 11.5 %collective-permute-start.4 = (f32[8,1,32,128]{3,2,1,0:T(8,128)S(1)}, f32[8,1,32,128]{3,2,1,0:T(8,128)S(1)}, u32[]{:S(2)}, u32[]{:S(2)}) collective-permute-start(f32[8,1,32,128]{3,2,1,0:T(8,128)S(1)} %get-tuple-element.572), channel_id=1, source_target_pairs={{8,0},{16,8},{24,16},{32,24},{40,32},{48,40},{56,48},{64,56},{72,6... | collective-permute-start | bytes 393224 | tf_op jit(solution)/shard_map/ppermute | solution.py:21
  128.5 5.6 %collective-permute-start.6 = (f32[8,16,1,128]{3,2,1,0:T(1,128)S(1)}, f32[8,16,1,128]{3,2,1,0:T(1,128)S(1)}, u32[]{:S(2)}, u32[]{:S(2)}) collective-permute-start(f32[8,16,1,128]{3,2,1,0:T(1,128)S(1)} %get-tuple-element.573), channel_id=1, source_target_pairs={{1,0},{2,1},{3,2},{4,3},{5,4},{6,5},{7,6},{9,8},{10,9},{11,10},{12... | collective-permute-start | bytes 196616 | tf_op jit(solution)/shard_map/ppermute | solution.py:21
  131.6 3.8 collective-permute-start.7
  137.6 11.2 %copy-start = (s32[1024]{0:T(1024)S(1)}, s32[1024]{0:T(1024)}, u32[]{:S(2)}) copy-start(s32[1024]{0:T(1024)} %param.19) | copy-start | bytes 12292
  138.8 9.9 %all-to-all-start = ((f32[16,2,128]{2,1,0:T(2,128)}), f32[16,2,128]{2,1,0:T(2,128)S(1)}, u32[]{:S(2)}, u32[]{:S(2)}) async-start(f32[16,2,128]{2,1,0:T(2,128)} %broadcast_select_fusion), calls=%async_computation | async-start | bytes 32768 | tf_op jit(solution)/shard_map/all_to_all | solution.py:174
  148.7 0.6 copy-start.2
  148.7 69.1 %all-gather.4.cloned.1.call-start = ((), (), s32[]{:S(2)}) async-start(), calls=%async_computation.1 | async-start | bytes 2113536 | tf_op jit(solution)/shard_map/while/body/eval_jaxpr/all_gather | solution.py:193
  161.5 58.9 %copy-start.3 = (f32[32,128]{1,0:T(8,128)S(1)}, f32[32,128]{1,0:T(8,128)}, u32[]{:S(2)}) copy-start(f32[32,128]{1,0:T(8,128)} %copy-done.2) | copy-start | bytes 49156 | tf_op jit(solution)/shard_map/while
  235.1 0.6 copy-start.2
  235.1 66.8 %all-gather.4.cloned.1.call-start = ((), (), s32[]{:S(2)}) async-start(), calls=%async_computation.1 | async-start | bytes 2113536 | tf_op jit(solution)/shard_map/while/body/eval_jaxpr/all_gather | solution.py:193
  247.9 56.6 %copy-start.3 = (f32[32,128]{1,0:T(8,128)S(1)}, f32[32,128]{1,0:T(8,128)}, u32[]{:S(2)}) copy-start(f32[32,128]{1,0:T(8,128)} %copy-done.2) | copy-start | bytes 49156 | tf_op jit(solution)/shard_map/while
  319.1 0.6 copy-start.2
  319.1 66.8 %all-gather.4.cloned.1.call-start = ((), (), s32[]{:S(2)}) async-start(), calls=%async_computation.1 | async-start | bytes 2113536 | tf_op jit(solution)/shard_map/while/body/eval_jaxpr/all_gather | solution.py:193
  332.0 56.6 %copy-start.3 = (f32[32,128]{1,0:T(8,128)S(1)}, f32[32,128]{1,0:T(8,128)}, u32[]{:S(2)}) copy-start(f32[32,128]{1,0:T(8,128)} %copy-done.2) | copy-start | bytes 49156 | tf_op jit(solution)/shard_map/while
  403.1 0.6 copy-start.2
  403.2 66.4 %all-gather.4.cloned.1.call-start = ((), (), s32[]{:S(2)}) async-start(), calls=%async_computation.1 | async-start | bytes 2113536 | tf_op jit(solution)/shard_map/while/body/eval_jaxpr/all_gather | solution.py:193
  415.9 56.4 %copy-start.3 = (f32[32,128]{1,0:T(8,128)S(1)}, f32[32,128]{1,0:T(8,128)}, u32[]{:S(2)}) copy-start(f32[32,128]{1,0:T(8,128)} %copy-done.2) | copy-start | bytes 49156 | tf_op jit(solution)/shard_map/while
  486.8 1.3 copy-start.1
Sparse Core Ops, SparseCore 0:
  152.7 65.1 all-gather.3
  239.1 62.7 all-gather.3
  323.1 62.7 all-gather.3
  406.8 62.7 all-gather.3
where the time goes:
time: 496 us; the launch traced here: 495 us
  waiting for transfers between devices  216 us (44%)
  local copies, waits for them, and re-layouts  79.7 us (16%)
  blocking collectives  64.4 us (13%)
  matrix products  58.2 us (12%)
  other arithmetic  36.2 us (7%)
  starting transfers between devices  26 us (5%)
  between operations  13.4 us (3%)
    all_gather x4, waiting for transfers between devices, one_panel(): every_slot = lax.all_gather(owner_rows, ('gx', 'gy'), axis=0, tiled=True)  209 us
    all_gather x1, blocking collectives, shards(): lax.all_gather(local_vals, ('gx', 'gy'), axis=0, tiled=True)  64.4 us
    dot_general x8, matrix products, regress(): jnp.dot(anomaly, spread.T, precision=PRECISE, preferred_element_type=jnp....  23.6 us
    dot_general x8, matrix products, regress(): jnp.dot(weighted * shrink[None, :], spread, precision=PRECISE, preferred_...  19.7 us
    dot_general x8, matrix products, regress(): jnp.dot(weighted, mean_gain[:, None], precision=PRECISE, preferred_elemen...  15 us
    gather x8, local copies, waits for them, and re-layouts, one_panel(): priors = every_slot[global_place[panel_index_list]]  14.7 us
    ppermute x4, starting transfers between devices, with_halo(): lax.ppermute(head, axis, [((i + 1) % count, i) for i in range(ends)])  14.7 us
  transfers between devices with their start and end apart: 13, of which 6 were waited for; matrix products, arithmetic and copies ran while one was open for 19% of the time, Pallas kernels for 0%

commit v1 on v0

--- a/solution.py
+++ b/solution.py
@@ -6,6 +6,11 @@
 FSTEPS = 2
 PANEL = 256
 PRECISE = lax.Precision.HIGHEST
+
+
+def gather_over(value, mesh_axis, dim):
+    repeated = jnp.stack([value] * lax.axis_size(mesh_axis))
+    return jnp.concatenate(lax.all_to_all(repeated, mesh_axis, 0, 0), axis=dim)
 
 
 def with_halo(cells, sides, width, closed):
@@ -190,7 +195,7 @@
     def one_panel(panel_num, carried):
         row_state, owner_rows = carried
         panel_index_list = lax.dynamic_slice_in_dim(obs_order, panel_num * PANEL, PANEL)
-        every_slot = lax.all_gather(owner_rows, ("gx", "gy"), axis=0, tiled=True)
+        every_slot = gather_over(owner_rows, ("gx", "gy"), 0)
         priors = every_slot[global_place[panel_index_list]]
         spread, mean_gain, shrink = panel_terms(
             priors, obs_vals[panel_index_list], obs_errs[panel_index_list]

time: 496 us -> 365 us (0.74)
  waiting for transfers between devices: 216 us -> 72.3 us
  starting transfers between devices: 26 us -> 51.3 us
  between operations: 13.4 us -> 0.37 us
    all_gather x4 -> x0, waiting for transfers between devices: 209 us -> none  [one_panel(): every_slot = lax.all_gather(owner_rows, ('gx', 'gy'), axis=0, tiled=True)]
    all_to_all x0 -> x4, waiting for transfers between devices: none -> 65.2 us  [gather_over(): return jnp.concatenate(lax.all_to_all(repeated, mesh_axis, 0, 0), axis=dim)]
    all_to_all x0 -> x4, starting transfers between devices: none -> 25.4 us  [gather_over(): return jnp.concatenate(lax.all_to_all(repeated, mesh_axis, 0, 0), axis=dim)]
    another operation x1 -> x5, local copies, waits for them, and re-layouts: 0.12 us -> 6.44 us  [the longest x4 6.32 us: gather_over(): repeated = jnp.stack([value] * lax.axis_size(mesh_axis))]
  transfers between devices with their start and end apart: 13 -> 13, of which waited for: 6 -> 6; matrix products, arithmetic and copies ran while one was open for 19% -> 25% of each run, Pallas kernels for 0% -> 0%
where the time goes in v1:
time: 365 us; the launch traced here: 364 us
  local copies, waits for them, and re-layouts  83.8 us (23%)
  waiting for transfers between devices  72.3 us (20%)
  blocking collectives  64.4 us (18%)
  matrix products  58.2 us (16%)
  starting transfers between devices  51.3 us (14%)
  other arithmetic  33.3 us (9%)
    all_to_all x4, waiting for transfers between devices, gather_over(): return jnp.concatenate(lax.all_to_all(repeated, mesh_axis, 0, 0), axis=dim)  65.2 us
    all_gather x1, blocking collectives, shards(): lax.all_gather(local_vals, ('gx', 'gy'), axis=0, tiled=True)  64.4 us
    all_to_all x4, starting transfers between devices, gather_over(): return jnp.concatenate(lax.all_to_all(repeated, mesh_axis, 0, 0), axis=dim)  25.4 us
    dot_general x8, matrix products, regress(): jnp.dot(anomaly, spread.T, precision=PRECISE, preferred_element_type=jnp....  23.6 us
    dot_general x8, matrix products, regress(): jnp.dot(weighted * shrink[None, :], spread, precision=PRECISE, preferred_...  19.7 us
    dot_general x8, matrix products, regress(): jnp.dot(weighted, mean_gain[:, None], precision=PRECISE, preferred_elemen...  15 us
    gather x8, local copies, waits for them, and re-layouts, one_panel(): priors = every_slot[global_place[panel_index_list]]  14.7 us
    ppermute x4, starting transfers between devices, with_halo(): lax.ppermute(head, axis, [((i + 1) % count, i) for i in range(ends)])  14.7 us
  transfers between devices with their start and end apart: 13, of which 6 were waited for; matrix products, arithmetic and copies ran while one was open for 25% of the time, Pallas kernels for 0%

profile of v1, /device:TPU:1, one launch (start us, length us, event | category | flops | bytes accessed | tf_op | source)
XLA Modules:
  0.0 364.2 jit_solution(5253012108497954847)
XLA Ops:
  1.3 3.3 collective-permute-start.2
  4.6 3.5 collective-permute-start.3
  10.5 3.8 %collective-permute-start = (f32[8,1,32,128]{3,2,1,0:T(8,128)S(1)}, f32[8,1,32,128]{3,2,1,0:T(8,128)S(1)}, u32[]{:S(2)}, u32[]{:S(2)}) collective-permute-start(f32[8,1,32,128]{3,2,1,0:T(8,128)S(1)} %get-tuple-element.576), channel_id=1, source_target_pairs={{8,0},{16,8},{24,16},{32,24},{40,32},{48,40},{56,48},{64,56},{72,6... | collective-permute-start | bytes 393224 | tf_op jit(solution)/shard_map/ppermute | solution.py:26
  16.5 4.4 %sort.34 = (s32[1024]{0:T(1024)}, s32[1024]{0:T(1024)S(1)}) sort(s32[1024]{0:T(1024)S(1)} %multiply_add_fusion.2, s32[1024]{0:T(1024)S(1)} %iota.44), dimensions={0}, to_apply=%region_0.1 | sort | flops 10240 | bytes 16384 | tf_op jit(solution)/shard_map/jit(argsort)/sort | solution.py:36
  20.8 4.5 %gather_fusion.8 = s32[1024]{0:T(1024)S(1)} fusion(s32[1024]{0:T(1024)S(1)} %multiply_add_fusion.2, s32[1024]{0:T(1024)S(1)} %fusion.51), kind=kCustom, calls=%fused_computation.8 | custom fusion | bytes 12288 | tf_op jit(solution)/shard_map/gather | solution.py:37
  25.5 4.4 %sort.35 = (s32[1024]{0:T(1024)}, s32[1024]{0:T(1024)S(1)}) sort(s32[1024]{0:T(1024)S(1)} %get-tuple-element.404, s32[1024]{0:T(1024)S(1)} %iota.50), dimensions={0}, to_apply=%region_3.4 | sort | flops 10240 | bytes 16384 | tf_op jit(solution)/shard_map/jit(argsort)/sort | solution.py:44
  30.5 4.5 %gather_fusion.9 = s32[1024]{0:T(1024)S(1)} fusion(s32[1024]{0:T(1024)S(1)} %get-tuple-element.585, s32[1024]{0:T(1024)S(1)} %get-tuple-element.584), kind=kCustom, calls=%fused_computation.9 | custom fusion | bytes 12288 | tf_op jit(solution)/shard_map/gather | solution.py:45
  37.1 64.4 %all-reduce.2 = (f32[4096]{0:T(1024)S(1)}, f32[4096]{0:T(1024)S(1)}) all-reduce(f32[4096]{0:T(1024)S(1)} %bitcast_dynamic-update-slice_fusion.1, f32[4096]{0:T(1024)S(1)} %bitcast_dynamic-update-slice_fusion), channel_id=2, replica_groups=mesh['gx'=16,'gy'=8] {'gx','gy'}, use_global_device_ids=true, to_apply=%add | all-reduce | flops 8192 | bytes 65536 | tf_op jit(solution)/shard_map/all_gather | solution.py:188
  101.5 6.1 %gather_fusion.12 = f32[1024]{0:T(1024)S(1)} fusion(f32[4096]{0:T(1024)S(1)} %get-tuple-element.561, s32[1024]{0:T(1024)S(1)} %get-tuple-element.564), kind=kCustom, calls=%fused_computation.12 | custom fusion | bytes 12288 | tf_op jit(solution)/shard_map/gather | solution.py:193
  107.7 6.2 %gather_fusion.11 = f32[1024]{0:T(1024)S(1)} fusion(f32[4096]{0:T(1024)S(1)} %get-tuple-element.560, s32[1024]{0:T(1024)S(1)} %get-tuple-element.564), kind=kCustom, calls=%fused_computation.11 | custom fusion | bytes 12288 | tf_op jit(solution)/shard_map/gather | solution.py:192
  114.8 2.2 multiply_subtract_fusion.1
  117.4 4.5 %collective-permute-start.4 = (f32[8,1,32,128]{3,2,1,0:T(8,128)S(1)}, f32[8,1,32,128]{3,2,1,0:T(8,128)S(1)}, u32[]{:S(2)}, u32[]{:S(2)}) collective-permute-start(f32[8,1,32,128]{3,2,1,0:T(8,128)S(1)} %get-tuple-element.572), channel_id=1, source_target_pairs={{8,0},{16,8},{24,16},{32,24},{40,32},{48,40},{56,48},{64,56},{72,6... | collective-permute-start | bytes 393224 | tf_op jit(solution)/shard_map/ppermute | solution.py:26
  122.0 3.1 collective-permute-start.6
  125.1 2.5 collective-permute-start.7
  128.9 2.1 multiply_subtract_fusion
  132.3 3.5 all-to-all-start.1
  136.4 5.8 %all-to-all-done.1 = f32[16,2,128]{2,1,0:T(2,128)S(1)} async-done(((f32[16,2,128]{2,1,0:T(2,128)}), f32[16,2,128]{2,1,0:T(2,128)S(1)}, u32[]{:S(2)}, u32[]{:S(2)}) %all-to-all-start.1) | async-done | bytes 16416 | tf_op jit(solution)/shard_map/all_to_all | solution.py:179
  142.2 220.7 %while.18 = (s32[]{:T(128)}, f32[4096,128]{1,0:T(8,128)S(1)}, f32[32,128]{1,0:T(8,128)S(1)}, s32[1024]{0:T(1024)}, s32[1024]{0:T(1024)S(1)}, /*index=5*/s32[1024...) while((s32[]{:T(128)}, f32[4096,128]{1,0:T(8,128)S(1)}, ...), condition=%wide.region_12.13_spmd.clone, body=%wide.region_7.12_spmd.clone.sunk | while | flops 3269761536 | bytes 38194076 | solution.py:221
  142.2 1.6 stack.8
  143.8 8.1 %all-to-all-start = ((f32[128,32,128]{2,1,0:T(8,128)}), f32[128,32,128]{2,1,0:T(8,128)}, u32[]{:S(2)}, u32[]{:S(2)}) async-start(f32[128,32,128]{2,1,0:T(8,128)} %stack.8), calls=%async_computation | async-start | bytes 4194304 | tf_op jit(solution)/shard_map/while/body/eval_jaxpr/all_to_all | solution.py:13
  152.8 1.4 gather_fusion.5
  154.2 1.4 gather_fusion.3
  155.5 1.4 gather_fusion.2
  156.9 1.4 gather_fusion.7
  158.3 1.4 gather_fusion.6
  159.7 1.4 gather_fusion.4
  161.0 1.4 gather_fusion
  163.3 2.3 broadcast_multiply_fusion.9
  165.6 16.2 %all-to-all-done = f32[128,32,128]{2,1,0:T(8,128)} async-done(((f32[128,32,128]{2,1,0:T(8,128)}), f32[128,32,128]{2,1,0:T(8,128)}, u32[]{:S(2)}, u32[]{:S(2)}) %all-to-all-start) | async-done | bytes 2097184 | tf_op jit(solution)/shard_map/while/body/eval_jaxpr/all_to_all | solution.py:13
  181.8 2.3 gather_fusion.1
  184.9 5.6 %fusion.99 = f32[4096,256]{1,0:T(8,128)S(1)} fusion(f32[4096,256]{1,0:T(8,128)} %bitcast.75, f32[4096,128]{1,0:T(8,128)S(1)} %get-tuple-element.720, f32[4096]{0:T(1024)S(1)} %broadcast_multiply_fusion.10, f32[256,128]{1,0:T(8,128)S(1)} %gather_fusion.1, f32[256]{0:T(256)S(1)} %broadcast_multiply_fusion.8), kind=kOutput, calls=%fused_computation.20.clone.1 | convolution fusion | flops 1613266944 | bytes 10634240 | tf_op jit(solution)/shard_map/while/body/eval_jaxpr/dot_general | solution.py:75
  190.5 3.6 fusion.100
  194.4 4.6 %fusion.102 = (f32[4096]{0:T(1024)S(1)}, f32[4096,128]{1,0:T(8,128)S(1)}) fusion(f32[256,128]{1,0:T(8,128)S(1)} %gather_fusion.1, f32[256]{0:T(256)S(1)} %broadcast_multiply_fusion.8, f32[4096,256]{1,0:T(8,128)S(1)} %fusion.99, f32[256]{0:T(256)S(1)} %get-tuple-element.693, f32[4096,128]{1,0:T(8,128)S(1)} %get-tuple-element.720, ...), kind=kOutput, calls=%fused_computation.162.clone.1 | convolution fusion | flops 1613787136 | bytes 8570880 | tf_op jit(solution)/shard_map/while/body/eval_jaxpr/dot_general | solution.py:82
  199.0 1.6 stack.8
  200.6 5.8 %all-to-all-start = ((f32[128,32,128]{2,1,0:T(8,128)}), f32[128,32,128]{2,1,0:T(8,128)}, u32[]{:S(2)}, u32[]{:S(2)}) async-start(f32[128,32,128]{2,1,0:T(8,128)} %stack.8), calls=%async_computation | async-start | bytes 4194304 | tf_op jit(solution)/shard_map/while/body/eval_jaxpr/all_to_all | solution.py:13
  207.3 1.4 gather_fusion.5
  208.7 1.4 gather_fusion.3
  210.0 1.4 gather_fusion.2
  211.4 1.4 gather_fusion.7
  212.8 1.4 gather_fusion.6
  217.8 2.3 broadcast_multiply_fusion.9
  220.1 16.3 %all-to-all-done = f32[128,32,128]{2,1,0:T(8,128)} async-done(((f32[128,32,128]{2,1,0:T(8,128)}), f32[128,32,128]{2,1,0:T(8,128)}, u32[]{:S(2)}, u32[]{:S(2)}) %all-to-all-start) | async-done | bytes 2097184 | tf_op jit(solution)/shard_map/while/body/eval_jaxpr/all_to_all | solution.py:13
  236.4 2.3 gather_fusion.1
  239.5 5.6 %fusion.99 = f32[4096,256]{1,0:T(8,128)S(1)} fusion(f32[4096,256]{1,0:T(8,128)} %bitcast.75, f32[4096,128]{1,0:T(8,128)S(1)} %get-tuple-element.720, f32[4096]{0:T(1024)S(1)} %broadcast_multiply_fusion.10, f32[256,128]{1,0:T(8,128)S(1)} %gather_fusion.1, f32[256]{0:T(256)S(1)} %broadcast_multiply_fusion.8), kind=kOutput, calls=%fused_computation.20.clone.1 | convolution fusion | flops 1613266944 | bytes 10634240 | tf_op jit(solution)/shard_map/while/body/eval_jaxpr/dot_general | solution.py:75
  245.1 3.6 fusion.100
  249.0 4.6 %fusion.102 = (f32[4096]{0:T(1024)S(1)}, f32[4096,128]{1,0:T(8,128)S(1)}) fusion(f32[256,128]{1,0:T(8,128)S(1)} %gather_fusion.1, f32[256]{0:T(256)S(1)} %broadcast_multiply_fusion.8, f32[4096,256]{1,0:T(8,128)S(1)} %fusion.99, f32[256]{0:T(256)S(1)} %get-tuple-element.693, f32[4096,128]{1,0:T(8,128)S(1)} %get-tuple-element.720, ...), kind=kOutput, calls=%fused_computation.162.clone.1 | convolution fusion | flops 1613787136 | bytes 8570880 | tf_op jit(solution)/shard_map/while/body/eval_jaxpr/dot_general | solution.py:82
  253.7 1.6 stack.8
  255.3 5.8 %all-to-all-start = ((f32[128,32,128]{2,1,0:T(8,128)}), f32[128,32,128]{2,1,0:T(8,128)}, u32[]{:S(2)}, u32[]{:S(2)}) async-start(f32[128,32,128]{2,1,0:T(8,128)} %stack.8), calls=%async_computation | async-start | bytes 4194304 | tf_op jit(solution)/shard_map/while/body/eval_jaxpr/all_to_all | solution.py:13
  261.9 1.4 gather_fusion.5
  272.4 2.3 broadcast_multiply_fusion.9
  274.7 16.3 %all-to-all-done = f32[128,32,128]{2,1,0:T(8,128)} async-done(((f32[128,32,128]{2,1,0:T(8,128)}), f32[128,32,128]{2,1,0:T(8,128)}, u32[]{:S(2)}, u32[]{:S(2)}) %all-to-all-start) | async-done | bytes 2097184 | tf_op jit(solution)/shard_map/while/body/eval_jaxpr/all_to_all | solution.py:13
  291.0 2.3 gather_fusion.1
  294.2 5.6 %fusion.99 = f32[4096,256]{1,0:T(8,128)S(1)} fusion(f32[4096,256]{1,0:T(8,128)} %bitcast.75, f32[4096,128]{1,0:T(8,128)S(1)} %get-tuple-element.720, f32[4096]{0:T(1024)S(1)} %broadcast_multiply_fusion.10, f32[256,128]{1,0:T(8,128)S(1)} %gather_fusion.1, f32[256]{0:T(256)S(1)} %broadcast_multiply_fusion.8), kind=kOutput, calls=%fused_computation.20.clone.1 | convolution fusion | flops 1613266944 | bytes 10634240 | tf_op jit(solution)/shard_map/while/body/eval_jaxpr/dot_general | solution.py:75
  299.7 3.6 fusion.100
  303.6 4.6 %fusion.102 = (f32[4096]{0:T(1024)S(1)}, f32[4096,128]{1,0:T(8,128)S(1)}) fusion(f32[256,128]{1,0:T(8,128)S(1)} %gather_fusion.1, f32[256]{0:T(256)S(1)} %broadcast_multiply_fusion.8, f32[4096,256]{1,0:T(8,128)S(1)} %fusion.99, f32[256]{0:T(256)S(1)} %get-tuple-element.693, f32[4096,128]{1,0:T(8,128)S(1)} %get-tuple-element.720, ...), kind=kOutput, calls=%fused_computation.162.clone.1 | convolution fusion | flops 1613787136 | bytes 8570880 | tf_op jit(solution)/shard_map/while/body/eval_jaxpr/dot_general | solution.py:82
  308.3 1.6 stack.8
  309.9 5.8 %all-to-all-start = ((f32[128,32,128]{2,1,0:T(8,128)}), f32[128,32,128]{2,1,0:T(8,128)}, u32[]{:S(2)}, u32[]{:S(2)}) async-start(f32[128,32,128]{2,1,0:T(8,128)} %stack.8), calls=%async_computation | async-start | bytes 4194304 | tf_op jit(solution)/shard_map/while/body/eval_jaxpr/all_to_all | solution.py:13
  323.4 1.4 gather_fusion.4
  327.0 2.3 broadcast_multiply_fusion.9
  329.3 16.3 %all-to-all-done = f32[128,32,128]{2,1,0:T(8,128)} async-done(((f32[128,32,128]{2,1,0:T(8,128)}), f32[128,32,128]{2,1,0:T(8,128)}, u32[]{:S(2)}, u32[]{:S(2)}) %all-to-all-start) | async-done | bytes 2097184 | tf_op jit(solution)/shard_map/while/body/eval_jaxpr/all_to_all | solution.py:13
  345.7 2.3 gather_fusion.1
  348.8 5.6 %fusion.99 = f32[4096,256]{1,0:T(8,128)S(1)} fusion(f32[4096,256]{1,0:T(8,128)} %bitcast.75, f32[4096,128]{1,0:T(8,128)S(1)} %get-tuple-element.720, f32[4096]{0:T(1024)S(1)} %broadcast_multiply_fusion.10, f32[256,128]{1,0:T(8,128)S(1)} %gather_fusion.1, f32[256]{0:T(256)S(1)} %broadcast_multiply_fusion.8), kind=kOutput, calls=%fused_computation.20.clone.1 | convolution fusion | flops 1613266944 | bytes 10634240 | tf_op jit(solution)/shard_map/while/body/eval_jaxpr/dot_general | solution.py:75
  354.4 3.6 fusion.100
  358.3 4.6 %fusion.102 = (f32[4096]{0:T(1024)S(1)}, f32[4096,128]{1,0:T(8,128)S(1)}) fusion(f32[256,128]{1,0:T(8,128)S(1)} %gather_fusion.1, f32[256]{0:T(256)S(1)} %broadcast_multiply_fusion.8, f32[4096,256]{1,0:T(8,128)S(1)} %fusion.99, f32[256]{0:T(256)S(1)} %get-tuple-element.693, f32[4096,128]{1,0:T(8,128)S(1)} %get-tuple-element.720, ...), kind=kOutput, calls=%fused_computation.162.clone.1 | convolution fusion | flops 1613787136 | bytes 8570880 | tf_op jit(solution)/shard_map/while/body/eval_jaxpr/dot_general | solution.py:82
  (178 shorter events, 44.6 us)
Async XLA Ops:
  1.3 113.3 %collective-permute-start.2 = (f32[8,16,1,128]{3,2,1,0:T(1,128)S(1)}, f32[8,16,1,128]{3,2,1,0:T(1,128)S(1)}, u32[]{:S(2)}, u32[]{:S(2)}) collective-permute-start(f32[8,16,1,128]{3,2,1,0:T(1,128)S(1)} %get-tuple-element.577), channel_id=1, source_target_pairs={{1,0},{2,1},{3,2},{4,3},{5,4},{6,5},{7,6},{9,8},{10,9},{11,10},{12... | collective-permute-start | bytes 196616 | tf_op jit(solution)/shard_map/ppermute | solution.py:26
  4.6 110.0 %collective-permute-start.3 = (f32[8,16,1,128]{3,2,1,0:T(1,128)S(1)}, f32[8,16,1,128]{3,2,1,0:T(1,128)S(1)}, u32[]{:S(2)}, u32[]{:S(2)}) collective-permute-start(f32[8,16,1,128]{3,2,1,0:T(1,128)S(1)} %get-tuple-element.578), channel_id=1, source_target_pairs={{0,1},{1,2},{2,3},{3,4},{4,5},{5,6},{6,7},{8,9},{9,10},{10,11},{11... | collective-permute-start | bytes 196616 | tf_op jit(solution)/shard_map/ppermute | solution.py:24
  9.2 105.5 %collective-permute-start.1 = (f32[8,1,32,128]{3,2,1,0:T(8,128)S(1)}, f32[8,1,32,128]{3,2,1,0:T(8,128)S(1)}, u32[]{:S(2)}, u32[]{:S(2)}) collective-permute-start(f32[8,1,32,128]{3,2,1,0:T(8,128)S(1)} %get-tuple-element.575), channel_id=1, source_target_pairs={{0,8},{8,16},{16,24},{24,32},{32,40},{40,48},{48,56},{56,64},{64,7... | collective-permute-start | bytes 393224 | tf_op jit(solution)/shard_map/ppermute | solution.py:24
  10.5 104.2 %collective-permute-start = (f32[8,1,32,128]{3,2,1,0:T(8,128)S(1)}, f32[8,1,32,128]{3,2,1,0:T(8,128)S(1)}, u32[]{:S(2)}, u32[]{:S(2)}) collective-permute-start(f32[8,1,32,128]{3,2,1,0:T(8,128)S(1)} %get-tuple-element.576), channel_id=1, source_target_pairs={{8,0},{16,8},{24,16},{32,24},{40,32},{48,40},{56,48},{64,56},{72,6... | collective-permute-start | bytes 393224 | tf_op jit(solution)/shard_map/ppermute | solution.py:26
  30.5 4.6 %copy-start.3 = (s32[1024]{0:T(1024)S(1)}, s32[1024]{0:T(1024)}, u32[]{:S(2)}) copy-start(s32[1024]{0:T(1024)} %param.20) | copy-start | bytes 12292
  30.5 4.6 %copy-start.7 = (s32[1024]{0:T(1024)S(1)}, s32[1024]{0:T(1024)}, u32[]{:S(2)}) copy-start(s32[1024]{0:T(1024)} %param.18) | copy-start | bytes 12292
  30.5 5.0 %copy-start.8 = (f32[1,1,32]{2,1,0:T(1,128)S(1)}, f32[1,1,32]{2,1,0:T(1,128)}, u32[]{:S(2)}) copy-start(f32[1,1,32]{2,1,0:T(1,128)} %param.22) | copy-start | bytes 388
  30.5 5.2 %copy-start.9 = (f32[1,1,32]{2,1,0:T(1,128)S(1)}, f32[1,1,32]{2,1,0:T(1,128)}, u32[]{:S(2)}) copy-start(f32[1,1,32]{2,1,0:T(1,128)} %param.23) | copy-start | bytes 388
  107.7 7.0 %copy-start.4 = (f32[4,16,32]{2,1,0:T(8,128)S(1)}, f32[4,16,32]{2,1,0:T(8,128)}, u32[]{:S(2)}) copy-start(f32[4,16,32]{2,1,0:T(8,128)} %param.14) | copy-start | bytes 24580
  107.7 7.0 %copy-start.5 = (f32[4,16,32]{2,1,0:T(8,128)S(1)}, f32[4,16,32]{2,1,0:T(8,128)}, u32[]{:S(2)}) copy-start(f32[4,16,32]{2,1,0:T(8,128)} %param.15) | copy-start | bytes 24580
  107.7 7.1 %copy-start.6 = (f32[4,16,32]{2,1,0:T(8,128)S(1)}, f32[4,16,32]{2,1,0:T(8,128)}, u32[]{:S(2)}) copy-start(f32[4,16,32]{2,1,0:T(8,128)} %param.16) | copy-start | bytes 24580
  107.7 7.1 %copy-start.2 = (f32[8,16,32,128]{3,2,1,0:T(8,128)S(1)}, f32[8,16,32,128]{3,2,1,0:T(8,128)}, u32[]{:S(2)}) copy-start(f32[8,16,32,128]{3,2,1,0:T(8,128)} %param.13) | copy-start | bytes 6291460
  117.0 11.8 %collective-permute-start.5 = (f32[8,1,32,128]{3,2,1,0:T(8,128)S(1)}, f32[8,1,32,128]{3,2,1,0:T(8,128)S(1)}, u32[]{:S(2)}, u32[]{:S(2)}) collective-permute-start(f32[8,1,32,128]{3,2,1,0:T(8,128)S(1)} %get-tuple-element.571), channel_id=1, source_target_pairs={{0,8},{8,16},{16,24},{24,32},{32,40},{40,48},{48,56},{56,64},{64,7... | collective-permute-start | bytes 393224 | tf_op jit(solution)/shard_map/ppermute | solution.py:24
  117.4 11.5 %collective-permute-start.4 = (f32[8,1,32,128]{3,2,1,0:T(8,128)S(1)}, f32[8,1,32,128]{3,2,1,0:T(8,128)S(1)}, u32[]{:S(2)}, u32[]{:S(2)}) collective-permute-start(f32[8,1,32,128]{3,2,1,0:T(8,128)S(1)} %get-tuple-element.572), channel_id=1, source_target_pairs={{8,0},{16,8},{24,16},{32,24},{40,32},{48,40},{56,48},{64,56},{72,6... | collective-permute-start | bytes 393224 | tf_op jit(solution)/shard_map/ppermute | solution.py:26
  122.0 5.6 %collective-permute-start.6 = (f32[8,16,1,128]{3,2,1,0:T(1,128)S(1)}, f32[8,16,1,128]{3,2,1,0:T(1,128)S(1)}, u32[]{:S(2)}, u32[]{:S(2)}) collective-permute-start(f32[8,16,1,128]{3,2,1,0:T(1,128)S(1)} %get-tuple-element.573), channel_id=1, source_target_pairs={{1,0},{2,1},{3,2},{4,3},{5,4},{6,5},{7,6},{9,8},{10,9},{11,10},{12... | collective-permute-start | bytes 196616 | tf_op jit(solution)/shard_map/ppermute | solution.py:26
  125.1 3.8 %collective-permute-start.7 = (f32[8,16,1,128]{3,2,1,0:T(1,128)S(1)}, f32[8,16,1,128]{3,2,1,0:T(1,128)S(1)}, u32[]{:S(2)}, u32[]{:S(2)}) collective-permute-start(f32[8,16,1,128]{3,2,1,0:T(1,128)S(1)} %get-tuple-element.574), channel_id=1, source_target_pairs={{0,1},{1,2},{2,3},{3,4},{4,5},{5,6},{6,7},{8,9},{9,10},{10,11},{11... | collective-permute-start | bytes 196616 | tf_op jit(solution)/shard_map/ppermute | solution.py:24
  131.0 11.2 %copy-start = (s32[1024]{0:T(1024)S(1)}, s32[1024]{0:T(1024)}, u32[]{:S(2)}) copy-start(s32[1024]{0:T(1024)} %param.19) | copy-start | bytes 12292
  132.3 9.9 %all-to-all-start.1 = ((f32[16,2,128]{2,1,0:T(2,128)}), f32[16,2,128]{2,1,0:T(2,128)S(1)}, u32[]{:S(2)}, u32[]{:S(2)}) async-start(f32[16,2,128]{2,1,0:T(2,128)} %broadcast_select_fusion), calls=%async_computation.1 | async-start | bytes 32768 | tf_op jit(solution)/shard_map/all_to_all | solution.py:179
  143.8 38.0 %all-to-all-start = ((f32[128,32,128]{2,1,0:T(8,128)}), f32[128,32,128]{2,1,0:T(8,128)}, u32[]{:S(2)}, u32[]{:S(2)}) async-start(f32[128,32,128]{2,1,0:T(8,128)} %stack.8), calls=%async_computation | async-start | bytes 4194304 | tf_op jit(solution)/shard_map/while/body/eval_jaxpr/all_to_all | solution.py:13
  200.6 35.8 %all-to-all-start = ((f32[128,32,128]{2,1,0:T(8,128)}), f32[128,32,128]{2,1,0:T(8,128)}, u32[]{:S(2)}, u32[]{:S(2)}) async-start(f32[128,32,128]{2,1,0:T(8,128)} %stack.8), calls=%async_computation | async-start | bytes 4194304 | tf_op jit(solution)/shard_map/while/body/eval_jaxpr/all_to_all | solution.py:13
  255.3 35.8 %all-to-all-start = ((f32[128,32,128]{2,1,0:T(8,128)}), f32[128,32,128]{2,1,0:T(8,128)}, u32[]{:S(2)}, u32[]{:S(2)}) async-start(f32[128,32,128]{2,1,0:T(8,128)} %stack.8), calls=%async_computation | async-start | bytes 4194304 | tf_op jit(solution)/shard_map/while/body/eval_jaxpr/all_to_all | solution.py:13
  309.9 35.8 %all-to-all-start = ((f32[128,32,128]{2,1,0:T(8,128)}), f32[128,32,128]{2,1,0:T(8,128)}, u32[]{:S(2)}, u32[]{:S(2)}) async-start(f32[128,32,128]{2,1,0:T(8,128)} %stack.8), calls=%async_computation | async-start | bytes 4194304 | tf_op jit(solution)/shard_map/while/body/eval_jaxpr/all_to_all | solution.py:13
  362.9 1.3 copy-start.1
